TPU v7x, 32 devices: a whole 2x2x4 slice. The times are simulated.
32 devices in a mesh: cell: 8 (over y, x, core), narrow: 4 (over z).
Axes of the slice: x: 2, y: 2, z: 4, core: 2. Of those that a mesh axis runs over, the one named last changes fastest.
Arguments:
- snapshots: bfloat16 [4096, 4096], P('cell', 'narrow'), may hold values from -6 to 6
- cell_volume: float32 [4096], P('cell'), may hold values from 0.1 to 10
- mode_vectors: bfloat16 [4096, 512], P('narrow'), may hold values from -0.09375 to 0.09375
- mode_scale: float32 [512], replicated, may hold values from 0.25 to 4
- interp_weights: bfloat16 [4096, 4096], P('cell', 'narrow'), may hold values from -0.09375 to 0.09375
Outputs:
- gram_matrix: float32 [4096, 4096], P('cell', 'narrow')
- fields: bfloat16 [4096, 4096], P('cell', 'narrow')
All inputs are finite; a program needn't handle non-finite values.
Results may differ from a plain program's by a relative error of at most 0.0064.
Values may be sent and summed in bfloat16 or wider, within the bound.
A program may use at most 128 MiB of HBM per device.

v0:
```python
import jax
import jax.numpy as jnp
from jax import lax
from jax.sharding import PartitionSpec as P


def shards(snapshots, cell_volume, mode_vectors, mode_scale, interp_weights):
    f32, bf16 = (jnp.float32, jnp.bfloat16)
    n_cell, n_narrow = (lax.axis_size("cell"), lax.axis_size("narrow"))
    total_cells = snapshots.shape[0] * n_cell
    rows = interp_weights.shape[0]
    weighted = (snapshots.astype(f32) * cell_volume[:, None]).astype(bf16)
    partial_shapes = jnp.dot(snapshots, mode_vectors, preferred_element_type=f32)
    mode_shapes = lax.psum(partial_shapes, "narrow").astype(bf16)
    gathered = lax.all_gather(snapshots, "narrow", axis=1, tiled=True)
    scaled_shapes = (
        mode_shapes.astype(f32) * (cell_volume / total_cells)[:, None] * mode_scale[None, :]
    ).astype(bf16)
    partial_coeffs = lax.dot_general(
        gathered, scaled_shapes, (((0,), (0,)), ((), ())), preferred_element_type=f32
    ).astype(bf16)
    coeffs = lax.psum_scatter(partial_coeffs, "cell", scatter_dimension=0, tiled=True)
    partial_new = lax.dot_general(
        coeffs, interp_weights, (((0,), (0,)), ((), ())), preferred_element_type=f32
    )
    new_coeffs = lax.psum(partial_new, "cell").astype(bf16)
    fields = jnp.dot(mode_shapes, new_coeffs, preferred_element_type=f32).astype(bf16)
    partial_gram = (
        lax.dot_general(gathered, weighted, (((0,), (0,)), ((), ())), preferred_element_type=f32)
        / total_cells
    ).astype(bf16)
    gram = lax.psum_scatter(partial_gram, "cell", scatter_dimension=0, tiled=True)
    return (gram.astype(f32), fields)


def solution(mesh):
    return jax.shard_map(
        shards,
        mesh=mesh,
        in_specs=(P("cell", "narrow"), P("cell"), P("narrow", None), P(), P("cell", "narrow")),
        out_specs=(P("cell", "narrow"), P("cell", "narrow")),
        check_vma=False,
    )
```

profile of v0, /device:TPU:0, one launch (start us, length us, event | category | flops | bytes accessed | tf_op | source)
XLA Modules:
  0.0 281.6 jit_solution(1832069264775600661)
XLA Ops:
  7.2 0.0 copy-start
  7.2 0.0 copy-start.4
  7.2 0.0 copy-start.3
  7.2 0.0 all-gather.2.cloned.1.call-start
  7.2 0.7 all-gather.2.cloned.1.call-update
  7.9 0.0 reduce-scatter.5.cloned.1.call-start
  8.0 2.2 fusion.8
  10.2 0.0 copy-done.4
  10.3 74.8 %all-reduce.2 = bf16[512,512]{1,0:T(8,128)(2,1)S(1)} all-reduce(f32[512,512]{1,0:T(8,128)S(1)} %fusion.8), channel_id=1, replica_groups=mesh['cell'=8,'narrow'=4] {'narrow'}, use_global_device_ids=true, to_apply=%region_1.0 | all-reduce | flops 262144 | bytes 1572864 | tf_op jit(solution)/shard_map/psum | solution.py:14
  85.1 0.0 copy-start.1
  85.1 34.5 %all-gather.2.cloned.1.call-done = bf16[512,4096]{1,0:T(8,128)(2,1)} async-done(((bf16[512,1024]{1,0:T(8,128)(2,1)}), bf16[512,4096]{1,0:T(8,128)(2,1)}) %all-gather.2.cloned.1.call-update) | async-done | bytes 4194320 | tf_op jit(solution)/shard_map/all_gather | solution.py:15
  119.6 0.0 copy-done.3
  119.6 6.6 %fusion.1 = bf16[4096,512]{0,1:T(8,128)(2,1)} fusion(bf16[512,4096]{1,0:T(8,128)(2,1)} %all-gather.2.cloned.1.call-done, f32[512]{0:T(512)S(1)} %copy-done.3, f32[512]{0:T(512)S(1)} %broadcast_multiply_fusion, bf16[512,512]{1,0:T(8,128)(2,1)S(1)} %all-reduce.2), kind=kOutput, calls=%fused_computation.3 | convolution fusion | flops 2150629376 | bytes 8916992 | tf_op jit(solution)/shard_map/dot_general | solution.py:19
  126.2 0.0 copy-done.1
  126.2 0.0 copy-start.2
  126.2 0.0 reduce-scatter.5.cloned.1.call-update
  126.3 0.0 reduce-scatter.3.cloned.1.call-start
  126.3 1.1 copy-done.2
  127.5 9.1 %fusion = bf16[4096,1024]{0,1:T(8,128)(2,1)} fusion(bf16[512,4096]{1,0:T(8,128)(2,1)} %all-gather.2.cloned.1.call-done, bf16[512,1024]{1,0:T(8,128)(2,1)S(1)} %copy-done.2, f32[512]{0:T(512)S(1)} %copy-done.4), kind=kOutput, calls=%fused_computation.1 | convolution fusion | flops 4304928768 | bytes 13633536 | tf_op jit(solution)/shard_map/dot_general | solution.py:29
  136.6 0.0 reduce-scatter.3.cloned.1.call-update
  136.6 41.2 %reduce-scatter.5.cloned.1.call-done = bf16[512,512]{0,1:T(8,128)(2,1)} async-done(((bf16[4096,512]{0,1:T(8,128)(2,1)}), bf16[512,512]{0,1:T(8,128)(2,1)}) %reduce-scatter.5.cloned.1.call-update) | async-done | bytes 524304 | tf_op jit(solution)/shard_map/reduce_scatter | solution.py:22
  177.8 0.0 copy-done
  177.8 1.8 fusion.9
  179.5 72.9 %all-reduce.3 = bf16[512,1024]{1,0:T(8,128)(2,1)} all-reduce(f32[512,1024]{1,0:T(8,128)S(1)} %fusion.9), channel_id=1, replica_groups=mesh['cell'=8,'narrow'=4] {'cell'}, use_global_device_ids=true, to_apply=%region_3.0 | all-reduce | flops 524288 | bytes 3145728 | tf_op jit(solution)/shard_map/psum | solution.py:26
  252.5 3.1 %convolution_convert_fusion.1 = bf16[512,1024]{1,0:T(8,128)(2,1)} fusion(bf16[512,1024]{1,0:T(8,128)(2,1)} %all-reduce.3, bf16[512,512]{1,0:T(8,128)(2,1)} %copy-done.1), kind=kOutput, calls=%fused_computation.5 | convolution fusion | flops 537395200 | bytes 2621440 | tf_op jit(solution)/shard_map/dot_general | solution.py:27
  255.5 16.9 %reduce-scatter.3.cloned.1.call-done = bf16[512,1024]{0,1:T(8,128)(2,1)} async-done(((bf16[4096,1024]{0,1:T(8,128)(2,1)}), bf16[512,1024]{0,1:T(8,128)(2,1)}) %reduce-scatter.3.cloned.1.call-update) | async-done | bytes 1048592 | tf_op jit(solution)/shard_map/reduce_scatter | solution.py:32
  272.5 2.6 copy.7
  (1 shorter events, 0.0 us)
Async XLA Ops:
  7.2 170.6 %copy-start = (bf16[512,1024]{1,0:T(8,128)(2,1)S(1)}, bf16[512,1024]{1,0:T(8,128)(2,1)}, u32[]{:S(2)}) copy-start(bf16[512,1024]{1,0:T(8,128)(2,1)} %param.9) | copy-start | bytes 3145732
  7.2 3.1 %copy-start.4 = (f32[512]{0:T(512)S(1)}, f32[512]{0:T(512)}, u32[]{:S(2)}) copy-start(f32[512]{0:T(512)} %param.6) | copy-start | bytes 6148
  7.2 112.4 %copy-start.3 = (f32[512]{0:T(512)S(1)}, f32[512]{0:T(512)}, u32[]{:S(2)}) copy-start(f32[512]{0:T(512)} %param.8) | copy-start | bytes 6148
  7.2 112.4 %all-gather.2.cloned.1.call-start = ((), (), s32[]{:S(2)}) async-start(), calls=%async_computation.2 | async-start | bytes 5242880 | tf_op jit(solution)/shard_map/all_gather | solution.py:15
  7.9 169.9 %reduce-scatter.5.cloned.1.call-start = ((), (), s32[]{:S(2)}) async-start(), calls=%async_computation.4 | async-start | bytes 4718592 | tf_op jit(solution)/shard_map/reduce_scatter | solution.py:22
  85.1 41.2 %copy-start.1 = (bf16[512,512]{1,0:T(8,128)(2,1)}, bf16[512,512]{1,0:T(8,128)(2,1)S(1)}, u32[]{:S(2)}) copy-start(bf16[512,512]{1,0:T(8,128)(2,1)S(1)} %all-reduce.2) | copy-start | bytes 1572868
  126.2 1.2 copy-start.2
  126.3 146.2 %reduce-scatter.3.cloned.1.call-start = ((), (), s32[]{:S(2)}) async-start(), calls=%async_computation.3 | async-start | bytes 9437184 | tf_op jit(solution)/shard_map/reduce_scatter | solution.py:32
Sparse Core Ops, SparseCore 0:
  9.6 109.9 all-gather.1
  126.4 51.3 reduce-scatter.4
  181.3 91.1 reduce-scatter.2
where the time goes:
time: 282 us
  blocking collectives  148 us (52%)
  waiting for transfers between devices  93.3 us (33%)
  matrix products  22.8 us (8%)
  between operations  13.8 us (5%)
  local copies, waits for them, and re-layouts  3.74 us (1%)
    psum x1, blocking collectives, shards(): mode_shapes = lax.psum(partial_shapes, 'narrow').astype(bf16)  74.8 us
    psum x1, blocking collectives, shards(): new_coeffs = lax.psum(partial_new, 'cell').astype(bf16)  72.9 us
    reduce_scatter x1, waiting for transfers between devices, shards(): lax.psum_scatter(partial_coeffs, 'cell', scatter_dimension=0, tiled=True)  41.2 us
    all_gather x1, waiting for transfers between devices, shards(): gathered = lax.all_gather(snapshots, 'narrow', axis=1, tiled=True)  34.5 us
    reduce_scatter x1, waiting for transfers between devices, shards(): lax.psum_scatter(partial_gram, 'cell', scatter_dimension=0, tiled=True)  16.9 us
    dot_general x1, matrix products, shards(): lax.dot_general(gathered, weighted, (((0,), (0,)), ((), ())), preferred_e...  9.13 us
    dot_general x1, matrix products, shards(): lax.dot_general(gathered, scaled_shapes, (((0,), (0,)), ((), ())), prefer...  6.61 us
  transfers between devices with their start and end apart: 3, of which 3 were waited for; matrix products, arithmetic and copies ran while one was open for 6% of the time, Pallas kernels for 0%

commit v1 on v0

--- a/solution.py
+++ b/solution.py
@@ -2,6 +2,12 @@
 import jax.numpy as jnp
 from jax import lax
 from jax.sharding import PartitionSpec as P
+
+
+def summed_here(x, axis):
+    shards = lax.all_gather(x, axis, axis=0, tiled=False)
+    total = shards.sum(axis=0)
+    return total
 
 
 def shards(snapshots, cell_volume, mode_vectors, mode_scale, interp_weights):
@@ -23,7 +29,7 @@
     partial_new = lax.dot_general(
         coeffs, interp_weights, (((0,), (0,)), ((), ())), preferred_element_type=f32
     )
-    new_coeffs = lax.psum(partial_new, "cell").astype(bf16)
+    new_coeffs = summed_here(partial_new, "cell").astype(bf16)
     fields = jnp.dot(mode_shapes, new_coeffs, preferred_element_type=f32).astype(bf16)
     partial_gram = (
         lax.dot_general(gathered, weighted, (((0,), (0,)), ((), ())), preferred_element_type=f32)

time: 282 us -> 361 us (1.28)
  waiting for transfers between devices: 93.3 us -> 237 us
  blocking collectives: 148 us -> 74.8 us
  other arithmetic: 0.01 us -> 7.94 us
    all_gather x0 -> x1, waiting for transfers between devices: none -> 88.9 us  [summed_here(): shards = lax.all_gather(x, axis, axis=0, tiled=False)]
    psum x1 -> x0, blocking collectives: 72.9 us -> none  [shards(): new_coeffs = lax.psum(partial_new, 'cell').astype(bf16)]
    reduce_scatter x1, waiting for transfers between devices: 16.9 us -> 71.6 us  [shards(): lax.psum_scatter(partial_gram, 'cell', scatter_dimension=0, tiled=True)]
    reduce_sum x0 -> x1, other arithmetic: none -> 7.94 us  [summed_here(): total = shards.sum(axis=0)]
  transfers between devices with their start and end apart: 3 -> 4, of which waited for: 3 -> 4; matrix products, arithmetic and copies ran while one was open for 6% -> 5% of each run, Pallas kernels for 0% -> 0%
where the time goes in v1:
time: 361 us; the launch traced here: 360 us
  waiting for transfers between devices  237 us (66%)
  blocking collectives  74.8 us (21%)
  matrix products  22.8 us (6%)
  between operations  13.8 us (4%)
  other arithmetic  7.94 us (2%)
  local copies, waits for them, and re-layouts  3.73 us (1%)
    all_gather x1, waiting for transfers between devices, summed_here(): shards = lax.all_gather(x, axis, axis=0, tiled=False)  88.9 us
    psum x1, blocking collectives, shards(): mode_shapes = lax.psum(partial_shapes, 'narrow').astype(bf16)  74.8 us
    reduce_scatter x1, waiting for transfers between devices, shards(): lax.psum_scatter(partial_gram, 'cell', scatter_dimension=0, tiled=True)  71.6 us
    reduce_scatter x1, waiting for transfers between devices, shards(): lax.psum_scatter(partial_coeffs, 'cell', scatter_dimension=0, tiled=True)  41.1 us
    all_gather x1, waiting for transfers between devices, shards(): gathered = lax.all_gather(snapshots, 'narrow', axis=1, tiled=True)  34.6 us
    dot_general x1, matrix products, shards(): lax.dot_general(gathered, weighted, (((0,), (0,)), ((), ())), preferred_e...  9.12 us
    reduce_sum x1, other arithmetic, summed_here(): total = shards.sum(axis=0)  7.94 us
  transfers between devices with their start and end apart: 4, of which 4 were waited for; matrix products, arithmetic and copies ran while one was open for 5% of the time, Pallas kernels for 0%

profile of v1, /device:TPU:0, one launch (start us, length us, event | category | flops | bytes accessed | tf_op | source)
XLA Modules:
  0.0 360.2 jit_solution(1477269806382173936)
XLA Ops:
  7.2 0.0 copy-start
  7.2 0.0 copy-start.3
  7.2 0.0 copy-start.2
  7.2 0.0 all-gather.4.cloned.1.call-start
  7.2 0.7 all-gather.4.cloned.1.call-update
  7.9 0.0 reduce-scatter.5.cloned.1.call-start
  8.0 2.2 fusion.8
  10.2 0.0 copy-done.3
  10.3 74.8 %all-reduce.1 = bf16[512,512]{1,0:T(8,128)(2,1)S(1)} all-reduce(f32[512,512]{1,0:T(8,128)S(1)} %fusion.8), channel_id=1, replica_groups=mesh['cell'=8,'narrow'=4] {'narrow'}, use_global_device_ids=true, to_apply=%region_1.0 | all-reduce | flops 262144 | bytes 1572864 | tf_op jit(solution)/shard_map/psum | solution.py:20
  85.1 34.6 %all-gather.4.cloned.1.call-done = bf16[512,4096]{1,0:T(8,128)(2,1)} async-done(((bf16[512,1024]{1,0:T(8,128)(2,1)}), bf16[512,4096]{1,0:T(8,128)(2,1)}) %all-gather.4.cloned.1.call-update) | async-done | bytes 4194320 | tf_op jit(solution)/shard_map/all_gather | solution.py:21
  119.6 0.0 copy-done.2
  119.6 6.6 %fusion.1 = bf16[4096,512]{0,1:T(8,128)(2,1)} fusion(bf16[512,4096]{1,0:T(8,128)(2,1)} %all-gather.4.cloned.1.call-done, f32[512]{0:T(512)S(1)} %copy-done.2, f32[512]{0:T(512)S(1)} %broadcast_multiply_fusion, bf16[512,512]{1,0:T(8,128)(2,1)S(1)} %all-reduce.1), kind=kOutput, calls=%fused_computation.3 | convolution fusion | flops 2150629376 | bytes 8916992 | tf_op jit(solution)/shard_map/dot_general | solution.py:25
  126.2 0.0 copy-start.1
  126.2 0.0 reduce-scatter.5.cloned.1.call-update
  126.3 0.0 reduce-scatter.3.cloned.1.call-start
  126.3 1.1 copy-done.1
  127.5 9.1 %fusion = bf16[4096,1024]{0,1:T(8,128)(2,1)} fusion(bf16[512,4096]{1,0:T(8,128)(2,1)} %all-gather.4.cloned.1.call-done, bf16[512,1024]{1,0:T(8,128)(2,1)S(1)} %copy-done.1, f32[512]{0:T(512)S(1)} %copy-done.3), kind=kOutput, calls=%fused_computation.1 | convolution fusion | flops 4304928768 | bytes 13633536 | tf_op jit(solution)/shard_map/dot_general | solution.py:35
  136.6 0.0 reduce-scatter.3.cloned.1.call-update
  136.6 0.0 all-gather.6.cloned.1.call-start
  136.7 41.1 %reduce-scatter.5.cloned.1.call-done = bf16[512,512]{0,1:T(8,128)(2,1)} async-done(((bf16[4096,512]{0,1:T(8,128)(2,1)}), bf16[512,512]{0,1:T(8,128)(2,1)}) %reduce-scatter.5.cloned.1.call-update) | async-done | bytes 524304 | tf_op jit(solution)/shard_map/reduce_scatter | solution.py:28
  177.8 0.0 copy-done
  177.8 3.1 fusion.9
  180.9 0.0 all-gather.6.cloned.1.call-update
  180.9 71.6 %reduce-scatter.3.cloned.1.call-done = bf16[512,1024]{0,1:T(8,128)(2,1)} async-done(((bf16[4096,1024]{0,1:T(8,128)(2,1)}), bf16[512,1024]{0,1:T(8,128)(2,1)}) %reduce-scatter.3.cloned.1.call-update) | async-done | bytes 1048592 | tf_op jit(solution)/shard_map/reduce_scatter | solution.py:38
  252.5 2.6 copy.7
  255.1 88.9 %all-gather.6.cloned.1.call-done = f32[4096,1024]{1,0:T(8,128)} async-done(((f32[512,1024]{1,0:T(8,128)}), f32[4096,1024]{1,0:T(8,128)}) %all-gather.6.cloned.1.call-update) | async-done | bytes 16777232 | tf_op jit(solution)/shard_map/all_gather | solution.py:8
  344.0 7.9 %reduce_sum.9 = bf16[512,1024]{1,0:T(8,128)(2,1)S(1)} reduce(f32[8,512,1024]{2,1,0:T(8,128)} %bitcast.13, f32[]{:T(128)} %constant.6.clone.1), dimensions={0}, to_apply=%region_3.0 | reduce | flops 3670016 | bytes 17825796 | tf_op jit(solution)/shard_map/reduce_sum | solution.py:9
  352.0 1.7 convolution_convert_fusion.1
  (1 shorter events, 0.0 us)
Async XLA Ops:
  7.2 170.6 %copy-start = (bf16[512,1024]{1,0:T(8,128)(2,1)S(1)}, bf16[512,1024]{1,0:T(8,128)(2,1)}, u32[]{:S(2)}) copy-start(bf16[512,1024]{1,0:T(8,128)(2,1)} %param.9) | copy-start | bytes 3145732
  7.2 3.1 copy-start.3
  7.2 112.4 %copy-start.2 = (f32[512]{0:T(512)S(1)}, f32[512]{0:T(512)}, u32[]{:S(2)}) copy-start(f32[512]{0:T(512)} %param.8) | copy-start | bytes 6148
  7.2 112.4 %all-gather.4.cloned.1.call-start = ((), (), s32[]{:S(2)}) async-start(), calls=%async_computation.2 | async-start | bytes 5242880 | tf_op jit(solution)/shard_map/all_gather | solution.py:21
  7.9 169.8 %reduce-scatter.5.cloned.1.call-start = ((), (), s32[]{:S(2)}) async-start(), calls=%async_computation.4 | async-start | bytes 4718592 | tf_op jit(solution)/shard_map/reduce_scatter | solution.py:28
  126.2 1.2 copy-start.1
  126.3 126.3 %reduce-scatter.3.cloned.1.call-start = ((), (), s32[]{:S(2)}) async-start(), calls=%async_computation.3 | async-start | bytes 9437184 | tf_op jit(solution)/shard_map/reduce_scatter | solution.py:38
  136.6 207.4 %all-gather.6.cloned.1.call-start = ((), (), s32[]{:S(2)}) async-start(), calls=%async_computation.5 | async-start | bytes 18874368 | tf_op jit(solution)/shard_map/all_gather | solution.py:8
Sparse Core Ops, SparseCore 0:
  9.6 109.9 all-gather.3
  126.4 51.3 reduce-scatter.4
  181.2 71.2 reduce-scatter.2
  254.3 89.6 all-gather.5
